TPU v7x, 128 devices: a whole 4x4x4 slice. The times are simulated.
128 devices in a mesh: ctx: 16 (over y, z_hi, core), head: 8 (over x, z_lo).
Axes of the slice: x: 4, y: 4, z: 4 (z_hi: 2, z_lo: 2; z = z_hi * 2 + z_lo), core: 2. Of those that a mesh axis runs over, the one named last changes fastest.
Arguments:
- queries: bfloat16 [2048, 12288], P('ctx', 'head'), may hold values from -8 to 8
- latents: bfloat16 [2048, 512], P('ctx'), may hold values from -4 to 4
- rope_key: bfloat16 [2048, 64], P('ctx'), may hold values from -8 to 8
- up_key_weight: bfloat16 [512, 8192], P(None, 'head'), may hold values from -0.5 to 0.5
- up_value_weight: bfloat16 [512, 8192], P(None, 'head'), may hold values from -0.25 to 0.25
- out_grad: bfloat16 [2048, 8192], P('ctx', 'head'), may hold values from -6 to 6
- group_order: int32 [32], replicated, may hold values from 0 to 31, as said below
Outputs:
- query_grad: bfloat16 [2048, 12288], P('ctx', 'head')
- latent_grad: float32 [2048, 512], P('ctx')
- rope_grad: float32 [2048, 64], P('ctx')
- up_key_grad: float32 [512, 8192], P('ctx', 'head')
- up_value_grad: float32 [512, 8192], P('ctx', 'head')
Inputs may be any that keep to these rules, and one draw needn't show every extreme that they name: A permutation of the 32 group numbers; storage slot k (rows k * 64 to k * 64 + 63) holds the sequence positions group_order[k] * 64 on, in order.
All inputs are finite; a program needn't handle non-finite values.
Results may differ from a plain program's by a relative error of at most 0.017.
Values may be sent and summed in bfloat16 or wider, within the bound.
No kernel may reach another device: no remote copies, remote signals or barrier semaphores. Data moves between devices by JAX's collectives and lax.ppermute only.
A program may use at most 64 MiB of HBM per device.

v0:
```python
import jax
import jax.numpy as jnp
from jax import lax
from jax.sharding import PartitionSpec as P

D_LATENT = 512
ROPE = 64
NOPE = 128
VDIM = 128
NEG_FILL = -1e30


def product(pattern, left_side, right_side):
    return jnp.einsum(pattern, left_side, right_side, preferred_element_type=jnp.float32)


def token_positions(group_order, row_ids, group_len):
    slot_ids = row_ids // group_len
    slot_table = jnp.arange(group_order.shape[0], dtype=jnp.int32)
    picked = jnp.sum(
        jnp.where(slot_ids[:, None] == slot_table[None, :], group_order[None, :], 0), axis=1
    )
    return picked * group_len + row_ids % group_len


def per_device(queries, latents, rope_key, up_key_weight, up_value_weight, out_grad, group_order):
    tok_count = queries.shape[0]
    head_count = up_key_weight.shape[1] // NOPE
    group_len = tok_count // 2
    scale_factor = (NOPE + ROPE) ** (-0.5)
    shaped = queries.reshape(tok_count, head_count, NOPE + ROPE)
    query_nope = shaped[:, :, :NOPE]
    query_rope = shaped[:, :, NOPE:]
    up_key = up_key_weight.reshape(D_LATENT, head_count, NOPE)
    up_value = up_value_weight.reshape(D_LATENT, head_count, VDIM)
    grad_out = out_grad.reshape(tok_count, head_count, VDIM)
    query_abs = product("thd,khd->thk", query_nope, up_key).astype(jnp.bfloat16)
    grad_lat = product("thd,khd->thk", grad_out, up_value).astype(jnp.bfloat16)
    own_rows = lax.axis_index("ctx") * tok_count + jnp.arange(tok_count, dtype=jnp.int32)
    query_pos = token_positions(group_order, own_rows, group_len)

    def piece_scores(latent_piece, rope_piece):
        scores = product("thk,nk->thn", query_abs, latent_piece) + product(
            "thr,nr->thn", query_rope, rope_piece
        )
        return scores * scale_factor

    latent_piece = lax.all_gather(latents, "ctx", axis=0, tiled=True)
    rope_piece = lax.all_gather(rope_key, "ctx", axis=0, tiled=True)
    row_count = latent_piece.shape[0]
    key_pos = token_positions(group_order, jnp.arange(row_count, dtype=jnp.int32), group_len)
    visible = key_pos[None, None, :] <= query_pos[:, None, None]
    run_max = jnp.full((tok_count, head_count), NEG_FILL, jnp.float32)
    scores = piece_scores(latent_piece, rope_piece)
    grad_prob = product("thk,nk->thn", grad_lat, latent_piece)
    new_max = jnp.maximum(run_max, jnp.max(jnp.where(visible, scores, NEG_FILL), axis=2))
    weights = jnp.where(visible, jnp.exp(scores - new_max[:, :, None]), 0.0)
    forward_state = (new_max, jnp.sum(weights, axis=2), jnp.sum(weights * grad_prob, axis=2))
    run_max, run_sum, run_dot = forward_state
    log_total = run_max + jnp.log(run_sum)
    row_delta = run_dot / run_sum
    latent_piece = lax.all_gather(latents, "ctx", axis=0, tiled=True)
    rope_piece = lax.all_gather(rope_key, "ctx", axis=0, tiled=True)
    row_count = latent_piece.shape[0]
    key_pos = token_positions(group_order, jnp.arange(row_count, dtype=jnp.int32), group_len)
    visible = key_pos[None, None, :] <= query_pos[:, None, None]
    scores = piece_scores(latent_piece, rope_piece)
    softmax_rows = jnp.where(visible, jnp.exp(scores - log_total[:, :, None]), 0.0)
    grad_prob = product("thk,nk->thn", grad_lat, latent_piece)
    grad_score = softmax_rows * (grad_prob - row_delta[:, :, None]) * scale_factor
    probs_low = softmax_rows.astype(jnp.bfloat16)
    grad_low = grad_score.astype(jnp.bfloat16)
    acc_out = product("thn,nk->thk", probs_low, latent_piece)
    acc_query = product("thn,nk->thk", grad_low, latent_piece)
    acc_rope = product("thn,nr->thr", grad_low, rope_piece)
    latent_part = product("thn,thk->nk", grad_low, query_abs) + product(
        "thn,thk->nk", probs_low, grad_lat
    )
    rope_part = product("thn,thr->nr", grad_low, query_rope)
    all_latent = latent_part
    all_rope = rope_part
    backward_state = (acc_query, acc_rope, acc_out, all_latent, all_rope)
    acc_query, acc_rope, acc_out, all_latent, all_rope = backward_state
    grad_abs = acc_query.astype(jnp.bfloat16)
    grad_nope = product("thk,khd->thd", grad_abs, up_key)
    query_grad = (
        jnp.concatenate([grad_nope, acc_rope], axis=2).astype(jnp.bfloat16).reshape(tok_count, -1)
    )
    out_low = acc_out.astype(jnp.bfloat16)
    weight_key_grad = product("thk,thd->khd", grad_abs, query_nope).reshape(D_LATENT, -1)
    weight_value_grad = product("thk,thd->khd", out_low, grad_out).reshape(D_LATENT, -1)
    up_key_grad, up_value_grad = (
        lax.psum_scatter(
            weight_key_grad.astype(jnp.bfloat16), "ctx", scatter_dimension=0, tiled=True
        ).astype(jnp.float32),
        lax.psum_scatter(
            weight_value_grad.astype(jnp.bfloat16), "ctx", scatter_dimension=0, tiled=True
        ).astype(jnp.float32),
    )
    partial_latent, partial_rope = (
        lax.psum_scatter(
            all_latent.astype(jnp.bfloat16), "ctx", scatter_dimension=0, tiled=True
        ).astype(jnp.float32),
        lax.psum_scatter(
            all_rope.astype(jnp.bfloat16), "ctx", scatter_dimension=0, tiled=True
        ).astype(jnp.float32),
    )
    latent_grad, rope_grad = (
        lax.psum(partial_latent.astype(jnp.bfloat16), "head").astype(jnp.float32),
        lax.psum(partial_rope.astype(jnp.bfloat16), "head").astype(jnp.float32),
    )
    return (query_grad, latent_grad, rope_grad, up_key_grad, up_value_grad)


def solution(mesh):
    placed = (
        P("ctx", "head"),
        P("ctx", None),
        P("ctx", None),
        P(None, "head"),
        P(None, "head"),
        P("ctx", "head"),
        P(),
    )
    return jax.shard_map(
        per_device,
        mesh=mesh,
        in_specs=placed,
        out_specs=(
            P("ctx", "head"),
            P("ctx", None),
            P("ctx", None),
            P("ctx", "head"),
            P("ctx", "head"),
        ),
        check_vma=False,
    )
```

profile of v0, /device:TPU:0, one launch (start us, length us, event | category | flops | bytes accessed | tf_op | source)
XLA Modules:
  0.0 446.0 jit_solution(16935749232204141822)
XLA Ops:
  7.2 0.0 all-gather.2.cloned.1.call-start
  7.2 0.7 all-gather.2.cloned.1.call-update
  7.9 0.0 reduce-scatter.7.cloned.1.call-start
  8.0 1.2 copy.63
  9.2 1.5 copy.90
  10.7 1.1 copy.91
  11.8 0.7 select_reduce_fusion.2
  12.6 0.8 select_reduce_fusion.1
  13.4 26.6 %all_gather.9 = bf16[2048,64]{0,1:T(8,128)(2,1)S(1)} all-gather(bf16[128,64]{0,1:T(8,128)(2,1)} %param.9), channel_id=1, replica_groups=mesh['ctx'=16,'head'=8] {'ctx'}, dimensions={0}, use_global_device_ids=true | all-gather | bytes 278528 | tf_op jit(solution)/shard_map/all_gather | solution.py:63
  40.0 1.5 fusion.18
  41.5 1.5 fusion.19
  42.9 0.2 broadcast_compare_fusion
  43.2 18.1 %all-gather.2.cloned.1.call-done = bf16[2048,512]{1,0:T(8,128)(2,1)} async-done(((bf16[128,512]{1,0:T(8,128)(2,1)}), bf16[2048,512]{1,0:T(8,128)(2,1)}) %all-gather.2.cloned.1.call-update) | async-done | bytes 2097168 | tf_op jit(solution)/shard_map/all_gather | solution.py:62
  61.3 4.3 fusion.10
  65.6 2.2 select_reduce_fusion
  67.9 4.3 fusion
  72.2 3.2 multiply_convert_fusion
  75.5 2.0 copy-done.1
  77.4 2.4 fusion.46
  79.9 4.7 %fusion.2 = bf16[2048,512]{1,0:T(8,128)(2,1)} fusion(f32[2048,512,1]{1,0,2:T(8,128)S(1)} %fusion.46, bf16[128,8,512]{0,2,1:T(8,128)(2,1)S(1)} %copy-done.6, f32[128,8,2048]{2,0,1:T(8,128)S(1)} %get-tuple-element.30, f32[128,8]{0,1:T(8,128)S(1)} %get-tuple-element.27, pred[128,2048]{1,0:T(8,128)(4,1)S(1)} %broadcast_compare_fusion), kind=kOutput, calls=%fused_computation.9 | convolution fusion | flops 2155872256 | bytes 15994880 | tf_op jit(solution)/shard_map/thn,thk->nk/dot_general | solution.py:14
  84.5 0.0 reduce-scatter.7.cloned.1.call-update
  84.6 0.0 reduce-scatter.13.cloned.1.call-start
  84.6 3.0 fusion.3
  87.7 1.0 copy.87
  88.7 0.0 reduce-scatter.13.cloned.1.call-update
  88.7 0.0 reduce-scatter.11.cloned.1.call-start
  88.8 7.7 %convolution_convert_fusion.1 = bf16[8,512,128]{1,2,0:T(8,128)(2,1)} fusion(bf16[128,8,128]{0,2,1:T(8,128)(2,1)S(1)} %bitcast.81, bf16[2048,512]{1,0:T(8,128)(2,1)} %all-gather.2.cloned.1.call-done, f32[128,8,2048]{2,0,1:T(8,128)} %copy-done.2, f32[128,8]{0,1:T(8,128)S(1)} %get-tuple-element.27, pred[128,2048]{1,0:T(8,128)(4,1)S(1)} %broadcast_compare_fusion), kind=kOutput, calls=%fused_computation.21 | convolution fusion | flops 2289041408 | bytes 12062720 | tf_op jit(solution)/shard_map/thk,thd->khd/dot_general | solution.py:14
  96.5 2.3 copy.78
  98.8 0.0 reduce-scatter.11.cloned.1.call-update
  98.8 0.3 reduce-scatter.9.cloned.1.call-start
  99.1 5.4 %fusion.12 = bf16[128,8,512]{2,0,1:T(8,128)(2,1)S(1)} fusion(bf16[128,8,2048]{2,0,1:T(8,128)(2,1)} %copy-done.1, bf16[2048,512]{1,0:T(8,128)(2,1)} %all-gather.2.cloned.1.call-done), kind=kOutput, calls=%fused_computation.24 | convolution fusion | flops 2148007936 | bytes 7340032 | tf_op jit(solution)/shard_map/thn,nk->thk/dot_general | solution.py:14
  104.5 1.4 convolution_convert_fusion
  105.9 2.4 copy.76
  108.2 0.0 all-reduce.2.cloned.1.call-start
  108.3 1.1 fusion.22
  109.4 3.6 convolution_convert_fusion.5
  113.1 41.4 %reduce-scatter.7.cloned.1.call-done = bf16[128,512]{1,0:T(8,128)(2,1)} async-done(((bf16[2048,512]{1,0:T(8,128)(2,1)}), bf16[128,512]{1,0:T(8,128)(2,1)}) %reduce-scatter.7.cloned.1.call-update) | async-done | bytes 131088 | tf_op jit(solution)/shard_map/reduce_scatter | solution.py:101
  154.6 0.9 copy.79
  155.5 67.5 %reduce-scatter.13.cloned.1.call-done = bf16[128,64]{1,0:T(8,128)(2,1)} async-done(((bf16[2048,64]{1,0:T(8,128)(2,1)}), bf16[128,64]{1,0:T(8,128)(2,1)}) %reduce-scatter.13.cloned.1.call-update) | async-done | bytes 16400
  223.0 0.8 copy.88
  223.8 33.4 %psum.15 = bf16[128,64]{0,1:T(8,128)(2,1)S(1)} all-reduce(bf16[128,64]{0,1:T(8,128)(2,1)S(1)} %copy.88), channel_id=1, replica_groups=mesh['ctx'=16,'head'=8] {'head'}, use_global_device_ids=true, to_apply=%region_8.9 | all-reduce | flops 8192 | bytes 32768 | tf_op jit(solution)/shard_map/psum | solution.py:110
  257.2 0.6 convert_element_type.80
  257.9 34.8 %reduce-scatter.11.cloned.1.call-done = bf16[32,1024]{1,0:T(8,128)(2,1)} async-done(((bf16[512,1024]{1,0:T(8,128)(2,1)}), bf16[32,1024]{1,0:T(8,128)(2,1)}) %reduce-scatter.11.cloned.1.call-update) | async-done | bytes 65552 | tf_op jit(solution)/shard_map/reduce_scatter | solution.py:96
  292.7 1.5 convert_element_type.89
  294.2 68.2 %reduce-scatter.9.cloned.1.call-done = bf16[32,1024]{1,0:T(8,128)(2,1)} async-done(((bf16[512,1024]{1,0:T(8,128)(2,1)}), bf16[32,1024]{1,0:T(8,128)(2,1)}) %reduce-scatter.9.cloned.1.call-update) | async-done | bytes 65552 | tf_op jit(solution)/shard_map/reduce_scatter | solution.py:93
  362.4 1.5 convert_element_type.84
  363.9 73.6 %all-reduce.2.cloned.1.call-done = bf16[128,512]{1,0:T(8,128)(2,1)} async-done(((bf16[128,512]{1,0:T(8,128)(2,1)}), bf16[128,512]{1,0:T(8,128)(2,1)}) %all-reduce.2.cloned.1.call-update) | async-done | bytes 131088 | tf_op jit(solution)/shard_map/psum | solution.py:109
  437.5 1.6 convert_element_type.78
  (26 shorter events, 0.1 us)
Async XLA Ops:
  7.2 34.3 %copy-start = (bf16[512,1024]{1,0:T(8,128)(2,1)S(1)}, bf16[512,1024]{1,0:T(8,128)(2,1)}, u32[]{:S(2)}) copy-start(bf16[512,1024]{1,0:T(8,128)(2,1)} %param.11) | copy-start | bytes 3145732
  7.2 54.1 %all-gather.2.cloned.1.call-start = ((), (), s32[]{:S(2)}) async-start(), calls=%async_computation.4 | async-start | bytes 2228224 | tf_op jit(solution)/shard_map/all_gather | solution.py:62
  7.9 146.6 %reduce-scatter.7.cloned.1.call-start = ((), (), s32[]{:S(2)}) async-start(), calls=%async_computation.5 | async-start | bytes 2228224 | tf_op jit(solution)/shard_map/reduce_scatter | solution.py:101
  39.9 25.7 %copy-start.3 = (bf16[2048,64]{0,1:T(8,128)(2,1)}, bf16[2048,64]{0,1:T(8,128)(2,1)S(1)}, u32[]{:S(2)}) copy-start(bf16[2048,64]{0,1:T(8,128)(2,1)S(1)} %all_gather.9) | copy-start | bytes 786436
  65.6 2.2 copy-start.6
  65.6 2.2 copy-start.8
  67.8 12.0 %copy-start.2 = (f32[128,8,2048]{2,0,1:T(8,128)}, f32[128,8,2048]{2,0,1:T(8,128)S(1)}, u32[]{:S(2)}) copy-start(f32[128,8,2048]{2,0,1:T(8,128)S(1)} %get-tuple-element.30) | copy-start | bytes 25165828
  72.2 5.2 %copy-start.7 = (bf16[128,8,512]{0,2,1:T(8,128)(2,1)S(1)}, bf16[128,8,512]{0,2,1:T(8,128)(2,1)}, u32[]{:S(2)}) copy-start(bf16[128,8,512]{0,2,1:T(8,128)(2,1)} %fusion.18) | copy-start | bytes 3145732
  75.5 2.0 copy-start.1
  84.6 138.4 %reduce-scatter.13.cloned.1.call-start = ((), (), s32[]{:S(2)}) async-start(), calls=%async_computation.9 | async-start | bytes 557056
  88.7 204.0 %reduce-scatter.11.cloned.1.call-start = ((), (), s32[]{:S(2)}) async-start(), calls=%async_computation.8 | async-start | bytes 1114112 | tf_op jit(solution)/shard_map/reduce_scatter | solution.py:96
  98.8 263.6 %reduce-scatter.9.cloned.1.call-start = ((), (), s32[]{:S(2)}) async-start(), calls=%async_computation.7 | async-start | bytes 1114112 | tf_op jit(solution)/shard_map/reduce_scatter | solution.py:93
  105.9 3.6 copy-start.4
  108.2 329.3 %all-reduce.2.cloned.1.call-start = ((), (), s32[]{:S(2)}) async-start(), calls=%async_computation.6 | async-start | bytes 262144 | tf_op jit(solution)/shard_map/psum | solution.py:109
  109.4 45.1 %copy-start.5 = (bf16[128,8,128]{0,2,1:T(8,128)(2,1)S(1)}, bf16[128,8,128]{0,2,1:T(8,128)(2,1)}, u32[]{:S(2)}) copy-start(bf16[128,8,128]{0,2,1:T(8,128)(2,1)} %fusion.22) | copy-start | bytes 786436
Sparse Core Ops, SparseCore 0:
  10.4 50.8 all-gather.1
  84.7 69.7 reduce-scatter.6
  158.3 64.6 reduce-scatter.12
  226.7 65.9 reduce-scatter.10
  296.4 65.9 reduce-scatter.8
  364.7 72.7 all-reduce.1
where the time goes:
time: 447 us; the launch traced here: 446 us
  waiting for transfers between devices  305 us (68%)
  blocking collectives  60 us (13%)
  matrix products  43.2 us (10%)
  between operations  14.3 us (3%)
  local copies, waits for them, and re-layouts  13.3 us (3%)
  other arithmetic  10.3 us (2%)
    psum x1, waiting for transfers between devices, per_device(): lax.psum(partial_latent.astype(jnp.bfloat16), 'head').astype(jnp.float32)  73.6 us
    unnamed x7, waiting for transfers between devices  68.2 us
    reduce_scatter x1, waiting for transfers between devices, per_device(): lax.psum_scatter(weight_key_grad.astype(jnp.bfloat16), 'ctx', scatter_dim...  68.2 us
    dot_general x13, matrix products, product(): jnp.einsum(pattern, left_side, right_side, preferred_element_type=jnp.flo...  43.2 us
    reduce_scatter x1, waiting for transfers between devices, per_device(): lax.psum_scatter(all_latent.astype(jnp.bfloat16), 'ctx', scatter_dimensio...  41.4 us
    reduce_scatter x1, waiting for transfers between devices, per_device(): lax.psum_scatter(weight_value_grad.astype(jnp.bfloat16), 'ctx', scatter_d...  34.8 us
    psum x1, blocking collectives, per_device(): lax.psum(partial_rope.astype(jnp.bfloat16), 'head').astype(jnp.float32)  33.4 us
    all_gather x1, blocking collectives, per_device(): rope_piece = lax.all_gather(rope_key, 'ctx', axis=0, tiled=True)  26.6 us
  transfers between devices with their start and end apart: 6, of which 6 were waited for; matrix products, arithmetic and copies ran while one was open for 9% of the time, Pallas kernels for 0%

commit v1 on v0

--- a/solution.py
+++ b/solution.py
@@ -106,7 +106,9 @@
         ).astype(jnp.float32),
     )
     latent_grad, rope_grad = (
-        lax.psum(partial_latent.astype(jnp.bfloat16), "head").astype(jnp.float32),
+        jnp.sum(lax.all_gather(partial_latent.astype(jnp.bfloat16), "head"), axis=0).astype(
+            jnp.float32
+        ),
         lax.psum(partial_rope.astype(jnp.bfloat16), "head").astype(jnp.float32),
     )
     return (query_grad, latent_grad, rope_grad, up_key_grad, up_value_grad)

time: 447 us -> 411 us (0.919)
  waiting for transfers between devices: 305 us -> 269 us
    psum x1 -> x0, waiting for transfers between devices: 73.6 us -> none  [per_device(): lax.psum(partial_latent.astype(jnp.bfloat16), 'head').astype(jnp.float32)]
    all_gather x0 -> x1, waiting for transfers between devices: none -> 37.8 us  [per_device(): lax.all_gather(partial_latent.astype(jnp.bfloat16), 'head')]
    reduce_scatter x1, waiting for transfers between devices: 41.4 us -> 46.2 us  [per_device(): lax.psum_scatter(all_latent.astype(jnp.bfloat16), 'ctx', scatter_dimensio...]
  transfers between devices with their start and end apart: 6 -> 6, of which waited for: 6 -> 6; matrix products, arithmetic and copies ran while one was open for 9% -> 10% of each run, Pallas kernels for 0% -> 0%
where the time goes in v1:
time: 411 us
  waiting for transfers between devices  269 us (65%)
  blocking collectives  60 us (15%)
  matrix products  42.4 us (10%)
  between operations  14.3 us (3%)
  local copies, waits for them, and re-layouts  13.3 us (3%)
  other arithmetic  10.7 us (3%)
    reduce_scatter x1, waiting for transfers between devices, per_device(): lax.psum_scatter(weight_key_grad.astype(jnp.bfloat16), 'ctx', scatter_dim...  68.2 us
    unnamed x7, waiting for transfers between devices  64.3 us
    reduce_scatter x1, waiting for transfers between devices, per_device(): lax.psum_scatter(all_latent.astype(jnp.bfloat16), 'ctx', scatter_dimensio...  46.2 us
    dot_general x13, matrix products, product(): jnp.einsum(pattern, left_side, right_side, preferred_element_type=jnp.flo...  42.4 us
    all_gather x1, waiting for transfers between devices, per_device(): lax.all_gather(partial_latent.astype(jnp.bfloat16), 'head')  37.8 us
    reduce_scatter x1, waiting for transfers between devices, per_device(): lax.psum_scatter(weight_value_grad.astype(jnp.bfloat16), 'ctx', scatter_d...  34.8 us
    psum x1, blocking collectives, per_device(): lax.psum(partial_rope.astype(jnp.bfloat16), 'head').astype(jnp.float32)  33.4 us
    all_gather x1, blocking collectives, per_device(): rope_piece = lax.all_gather(rope_key, 'ctx', axis=0, tiled=True)  26.6 us
  transfers between devices with their start and end apart: 6, of which 6 were waited for; matrix products, arithmetic and copies ran while one was open for 10% of the time, Pallas kernels for 0%

profile of v1, /device:TPU:0, one launch (start us, length us, event | category | flops | bytes accessed | tf_op | source)
XLA Modules:
  0.0 410.7 jit_solution(9511381442061965321)
XLA Ops:
  7.2 0.0 all-gather.4.cloned.1.call-start
  7.2 0.7 all-gather.4.cloned.1.call-update
  7.9 0.0 reduce-scatter.7.cloned.1.call-start
  8.0 1.2 copy.63
  9.2 1.5 copy.90
  10.7 1.1 copy.91
  11.9 0.7 select_reduce_fusion.2
  12.6 0.8 select_reduce_fusion.1
  13.4 26.6 %all_gather.15 = bf16[2048,64]{0,1:T(8,128)(2,1)S(1)} all-gather(bf16[128,64]{0,1:T(8,128)(2,1)} %param.9), channel_id=1, replica_groups=mesh['ctx'=16,'head'=8] {'ctx'}, dimensions={0}, use_global_device_ids=true | all-gather | bytes 278528 | tf_op jit(solution)/shard_map/all_gather | solution.py:63
  40.0 1.5 fusion.18
  41.5 1.5 fusion.19
  42.9 0.2 broadcast_compare_fusion
  43.2 18.1 %all-gather.4.cloned.1.call-done = bf16[2048,512]{1,0:T(8,128)(2,1)} async-done(((bf16[128,512]{1,0:T(8,128)(2,1)}), bf16[2048,512]{1,0:T(8,128)(2,1)}) %all-gather.4.cloned.1.call-update) | async-done | bytes 2097168 | tf_op jit(solution)/shard_map/all_gather | solution.py:62
  61.3 4.3 %fusion.10 = f32[128,8,2048]{2,0,1:T(8,128)S(1)} fusion(bf16[128,8,512]{0,2,1:T(8,128)(2,1)} %fusion.18, bf16[2048,512]{1,0:T(8,128)(2,1)} %all-gather.4.cloned.1.call-done), kind=kOutput, calls=%fused_computation.18 | convolution fusion | flops 2147483648 | bytes 11534336 | tf_op jit(solution)/shard_map/thk,nk->thn/dot_general | solution.py:14
  65.6 2.2 select_reduce_fusion
  67.9 4.3 %fusion = (f32[128,8]{0,1:T(8,128)S(1)}, f32[128,8]{0,1:T(8,128)S(1)}, f32[128,8,2048]{2,0,1:T(8,128)S(1)}) fusion(f32[128,8,2048]{2,0,1:T(8,128)S(1)} %get-tuple-element.30, f32[128,8]{0,1:T(8,128)S(1)} %broadcast_maximum_fusion, pred[128,2048]{1,0:T(8,128)(4,1)S(1)} %broadcast_compare_fusion, bf16[128,8,512]{0,2,1:T(8,128)(2,1)S(1)} %copy-done.5, ...), kind=kOutput, calls=%fused_computation.6 | convolution fusion | flops 2157967360 | bytes 20197376 | tf_op jit(solution)/shard_map/thk,nk->thn/dot_general | solution.py:14
  72.2 3.2 multiply_convert_fusion
  75.5 2.0 copy-done.1
  77.4 2.4 fusion.46
  79.9 4.7 %fusion.2 = bf16[2048,512]{1,0:T(8,128)(2,1)} fusion(f32[2048,512,1]{1,0,2:T(8,128)S(1)} %fusion.46, bf16[128,8,512]{0,2,1:T(8,128)(2,1)S(1)} %copy-done.5, f32[128,8,2048]{2,0,1:T(8,128)S(1)} %get-tuple-element.30, f32[128,8]{0,1:T(8,128)S(1)} %get-tuple-element.27, pred[128,2048]{1,0:T(8,128)(4,1)S(1)} %broadcast_compare_fusion), kind=kOutput, calls=%fused_computation.9 | convolution fusion | flops 2155872256 | bytes 15994880 | tf_op jit(solution)/shard_map/thn,thk->nk/dot_general | solution.py:14
  84.5 0.0 reduce-scatter.7.cloned.1.call-update
  84.6 0.0 reduce-scatter.13.cloned.1.call-start
  84.6 3.0 fusion.3
  87.7 1.0 copy.87
  88.7 0.0 reduce-scatter.13.cloned.1.call-update
  88.7 0.0 reduce-scatter.11.cloned.1.call-start
  88.8 7.7 %convolution_convert_fusion.1 = bf16[8,512,128]{1,2,0:T(8,128)(2,1)} fusion(bf16[128,8,128]{0,2,1:T(8,128)(2,1)S(1)} %bitcast.82, bf16[2048,512]{1,0:T(8,128)(2,1)} %all-gather.4.cloned.1.call-done, f32[128,8,2048]{2,0,1:T(8,128)} %copy-done.2, f32[128,8]{0,1:T(8,128)S(1)} %get-tuple-element.27, pred[128,2048]{1,0:T(8,128)(4,1)S(1)} %broadcast_compare_fusion), kind=kOutput, calls=%fused_computation.21 | convolution fusion | flops 2289041408 | bytes 12062720 | tf_op jit(solution)/shard_map/thk,thd->khd/dot_general | solution.py:14
  96.5 2.3 copy.78
  98.8 0.3 reduce-scatter.9.cloned.1.call-start
  99.1 5.4 %fusion.12 = bf16[128,8,512]{2,0,1:T(8,128)(2,1)S(1)} fusion(bf16[128,8,2048]{2,0,1:T(8,128)(2,1)} %copy-done.1, bf16[2048,512]{1,0:T(8,128)(2,1)} %all-gather.4.cloned.1.call-done), kind=kOutput, calls=%fused_computation.24 | convolution fusion | flops 2148007936 | bytes 7340032 | tf_op jit(solution)/shard_map/thn,nk->thk/dot_general | solution.py:14
  104.5 1.4 convolution_convert_fusion
  105.9 2.4 copy.76
  108.3 0.0 all-gather.6.cloned.1.call-start
  108.3 46.2 %reduce-scatter.7.cloned.1.call-done = bf16[128,512]{1,0:T(8,128)(2,1)} async-done(((bf16[2048,512]{1,0:T(8,128)(2,1)}), bf16[128,512]{1,0:T(8,128)(2,1)}) %reduce-scatter.7.cloned.1.call-update) | async-done | bytes 131088 | tf_op jit(solution)/shard_map/reduce_scatter | solution.py:101
  154.5 0.4 fusion.22
  155.0 3.6 convolution_convert_fusion.5
  158.6 0.9 copy.79
  159.5 63.5 %reduce-scatter.13.cloned.1.call-done = bf16[128,64]{1,0:T(8,128)(2,1)} async-done(((bf16[2048,64]{1,0:T(8,128)(2,1)}), bf16[128,64]{1,0:T(8,128)(2,1)}) %reduce-scatter.13.cloned.1.call-update) | async-done | bytes 16400
  223.1 0.8 copy.88
  223.9 33.4 %psum.7 = bf16[128,64]{0,1:T(8,128)(2,1)S(1)} all-reduce(bf16[128,64]{0,1:T(8,128)(2,1)S(1)} %copy.88), channel_id=1, replica_groups=mesh['ctx'=16,'head'=8] {'head'}, use_global_device_ids=true, to_apply=%region_8.9 | all-reduce | flops 8192 | bytes 32768 | tf_op jit(solution)/shard_map/psum | solution.py:112
  257.3 0.6 convert_element_type.82
  257.9 34.8 %reduce-scatter.11.cloned.1.call-done = bf16[32,1024]{1,0:T(8,128)(2,1)} async-done(((bf16[512,1024]{1,0:T(8,128)(2,1)}), bf16[32,1024]{1,0:T(8,128)(2,1)}) %reduce-scatter.11.cloned.1.call-update) | async-done | bytes 65552 | tf_op jit(solution)/shard_map/reduce_scatter | solution.py:96
  292.7 1.5 convert_element_type.91
  294.2 68.2 %reduce-scatter.9.cloned.1.call-done = bf16[32,1024]{1,0:T(8,128)(2,1)} async-done(((bf16[512,1024]{1,0:T(8,128)(2,1)}), bf16[32,1024]{1,0:T(8,128)(2,1)}) %reduce-scatter.9.cloned.1.call-update) | async-done | bytes 65552 | tf_op jit(solution)/shard_map/reduce_scatter | solution.py:93
  362.4 1.5 convert_element_type.86
  363.9 37.8 %all-gather.6.cloned.1.call-done = bf16[1024,512]{1,0:T(8,128)(2,1)} async-done(((bf16[128,512]{1,0:T(8,128)(2,1)}), bf16[1024,512]{1,0:T(8,128)(2,1)}) %all-gather.6.cloned.1.call-update) | async-done | bytes 1048592 | tf_op jit(solution)/shard_map/all_gather | solution.py:109
  401.7 1.4 reduce_sum.56
  403.1 0.7 convert_element_type.80
  (25 shorter events, 0.2 us)
Async XLA Ops:
  7.2 34.3 %copy-start = (bf16[512,1024]{1,0:T(8,128)(2,1)S(1)}, bf16[512,1024]{1,0:T(8,128)(2,1)}, u32[]{:S(2)}) copy-start(bf16[512,1024]{1,0:T(8,128)(2,1)} %param.11) | copy-start | bytes 3145732
  7.2 54.1 %all-gather.4.cloned.1.call-start = ((), (), s32[]{:S(2)}) async-start(), calls=%async_computation.4 | async-start | bytes 2228224 | tf_op jit(solution)/shard_map/all_gather | solution.py:62
  7.9 146.6 %reduce-scatter.7.cloned.1.call-start = ((), (), s32[]{:S(2)}) async-start(), calls=%async_computation.5 | async-start | bytes 2228224 | tf_op jit(solution)/shard_map/reduce_scatter | solution.py:101
  39.9 25.7 %copy-start.3 = (bf16[2048,64]{0,1:T(8,128)(2,1)}, bf16[2048,64]{0,1:T(8,128)(2,1)S(1)}, u32[]{:S(2)}) copy-start(bf16[2048,64]{0,1:T(8,128)(2,1)S(1)} %all_gather.15) | copy-start | bytes 786436
  65.6 2.2 copy-start.5
  65.6 2.2 copy-start.7
  67.8 12.0 %copy-start.2 = (f32[128,8,2048]{2,0,1:T(8,128)}, f32[128,8,2048]{2,0,1:T(8,128)S(1)}, u32[]{:S(2)}) copy-start(f32[128,8,2048]{2,0,1:T(8,128)S(1)} %get-tuple-element.30) | copy-start | bytes 25165828
  72.2 5.2 %copy-start.6 = (bf16[128,8,512]{0,2,1:T(8,128)(2,1)S(1)}, bf16[128,8,512]{0,2,1:T(8,128)(2,1)}, u32[]{:S(2)}) copy-start(bf16[128,8,512]{0,2,1:T(8,128)(2,1)} %fusion.18) | copy-start | bytes 3145732
  75.5 2.0 copy-start.1
  84.6 138.5 %reduce-scatter.13.cloned.1.call-start = ((), (), s32[]{:S(2)}) async-start(), calls=%async_computation.9 | async-start | bytes 557056
  88.7 204.0 %reduce-scatter.11.cloned.1.call-start = ((), (), s32[]{:S(2)}) async-start(), calls=%async_computation.7 | async-start | bytes 1114112 | tf_op jit(solution)/shard_map/reduce_scatter | solution.py:96
  98.8 263.6 %reduce-scatter.9.cloned.1.call-start = ((), (), s32[]{:S(2)}) async-start(), calls=%async_computation.6 | async-start | bytes 1114112 | tf_op jit(solution)/shard_map/reduce_scatter | solution.py:93
  105.9 49.1 %copy-start.4 = (bf16[2048,64]{0,1:T(8,128)(2,1)S(1)}, bf16[2048,64]{0,1:T(8,128)(2,1)}, u32[]{:S(2)}) copy-start(bf16[2048,64]{0,1:T(8,128)(2,1)} %copy-done.3) | copy-start | bytes 786436
  108.3 293.5 %all-gather.6.cloned.1.call-start = ((), (), s32[]{:S(2)}) async-start(), calls=%async_computation.8 | async-start | bytes 1179648 | tf_op jit(solution)/shard_map/all_gather | solution.py:109
Sparse Core Ops, SparseCore 0:
  10.4 50.8 all-gather.3
  84.7 69.7 reduce-scatter.6
  158.3 64.7 reduce-scatter.12
  226.7 65.9 reduce-scatter.10
  296.4 65.9 reduce-scatter.8
  363.9 37.7 all-gather.5
